TPU v7x, 32 devices: a whole 2x2x4 slice. The times are simulated.
32 devices in a mesh: lvl: 2 (over x), lat: 4 (over z), lon: 4 (over y, core).
Axes of the slice: x: 2, y: 2, z: 4, core: 2. Of those that a mesh axis runs over, the one named last changes fastest.
Arguments:
- patches: bfloat16 [2, 2, 24, 48, 1000], P('lvl', None, 'lat', 'lon'), may hold values from -6 to 6
- level_embed: float32 [2, 512], P('lvl'), may hold values from -6 to 6
- embed_weight: bfloat16 [1000, 512], replicated, may hold values from -0.1875 to 0.1875
- block_ids: int32 [2, 2, 4, 4, 3], P('lvl', None, 'lat', 'lon'), may hold values from -1 to 5, as said below
- latent_queries: bfloat16 [4, 512], replicated, may hold values from -6 to 6
- cross_gain: float32 [512], replicated, may hold values from 0.1 to 1.9
- cross_query: bfloat16 [512, 512], replicated, may hold values from -0.25 to 0.25
- cross_kv: bfloat16 [512, 1024], replicated, may hold values from -0.25 to 0.25
- cross_out: bfloat16 [512, 512], replicated, may hold values from -0.25 to 0.25
- region_ids: int32 [48, 48], P(('lvl', 'lat'), 'lon'), may hold values from 0 to 2
- swin_gain: float32 [512], replicated, may hold values from 0.1 to 1.9
- swin_qkv: bfloat16 [512, 1536], replicated, may hold values from -0.25 to 0.25
- swin_out: bfloat16 [512, 512], replicated, may hold values from -0.25 to 0.25
- mlp_gain: float32 [512], replicated, may hold values from 0.1 to 1.9
- mlp_up: bfloat16 [512, 2048], replicated, may hold values from -0.25 to 0.25
- mlp_down: bfloat16 [2048, 512], replicated, may hold values from -0.125 to 0.125
Outputs:
- latents: float32 [4, 48, 48, 512], P(None, ('lvl', 'lat'), 'lon')
Inputs may be any that keep to these rules, and one draw needn't show every extreme that they name: block_ids[l, m, a, o, :] lists the column blocks b (longitude column (m * 4 + a) * 6 + b, latitude rows o * 12 to o * 12 + 11) at which level l is present: distinct numbers in its first slots, -1 in the remaining slots. Every column block is named by the list of at least one level. For every band and tile, the list of some level fills all 3 slots.
All inputs are finite; a program needn't handle non-finite values.
Results may differ from a plain program's by a relative error of at most 0.005.
Values may be sent and summed in bfloat16 or wider, within the bound.
A program may use at most 64 MiB of HBM per device.

v0:
```python
import math

import jax
import jax.numpy as jnp
from jax import lax
from jax.sharding import PartitionSpec as P

HEADS = 16
WIN_LV = 2
WIN_LAT = 6


def from_partner(block, axis, distance):
    count = lax.axis_size(axis)
    route = []
    for low in range(count):
        high = low | 1 << distance
        if high != low and high < count:
            route += [(low, high), (high, low)]
    return lax.ppermute(block, axis, route)


def with_halo(block, sides, width):
    for axis, dim in sides:
        count = lax.axis_size(axis)
        forward = [(i, i + 1) for i in range(count - 1)]
        backward = [(target, source) for source, target in forward]
        low = lax.ppermute(
            lax.slice_in_dim(block, block.shape[dim] - width, None, axis=dim), axis, forward
        )
        high = lax.ppermute(lax.slice_in_dim(block, 0, width, axis=dim), axis, backward)
        block = jnp.concatenate([low, block, high], axis=dim)
    return block


def layer_norm(tensor, gain_vec):
    average = jnp.mean(tensor, axis=-1, keepdims=True)
    centred = tensor - average
    spread = jnp.mean(centred * centred, axis=-1, keepdims=True)
    return centred * lax.rsqrt(spread + 1e-05) * gain_vec


def to_windows(tensor, spans):
    trailing = tensor.shape[3:]
    level_span, row_span, col_span = tensor.shape[:3]
    first, second, third = spans
    shaped = tensor.reshape(
        (level_span // first, first, row_span // second, second, col_span // third, third)
        + trailing
    )
    axes_order = (0, 2, 4, 1, 3, 5) + tuple(range(6, 6 + len(trailing)))
    return shaped.transpose(axes_order).reshape(
        (level_span // first, row_span // second, col_span // third, first * second * third)
        + trailing
    )


def from_windows(tensor, extents, spans):
    trailing = tensor.shape[4:]
    level_span, row_span, col_span = extents
    first, second, third = spans
    shaped = tensor.reshape(
        (level_span // first, row_span // second, col_span // third, first, second, third)
        + trailing
    )
    axes_order = (0, 3, 1, 4, 2, 5) + tuple(range(6, 6 + len(trailing)))
    return shaped.transpose(axes_order).reshape((level_span, row_span, col_span) + trailing)


def label_windows(labels, spans):
    row_span, col_span = labels.shape
    second, third = spans
    shaped = labels.reshape(row_span // second, second, col_span // third, third).transpose(
        0, 2, 1, 3
    )
    shaped = shaped.reshape(row_span // second, col_span // third, second * third)
    return jnp.concatenate([shaped] * WIN_LV, axis=-1)


def window_attend(queries, key_rows, value_rows, allowed, head_mask):
    masked = queries[:, :, :, None] * head_mask[:, None, :]
    scores = jnp.einsum(
        "abchqd,abckd->abchqk", masked, key_rows, preferred_element_type=jnp.float32
    )
    exponent = jnp.where(allowed[:, :, :, None], jnp.exp(scores), jnp.zeros_like(scores))
    weights = (exponent / jnp.sum(exponent, axis=-1, keepdims=True)).astype(jnp.bfloat16)
    mixture = jnp.einsum(
        "abchqk,abckd->abchqd", weights, value_rows, preferred_element_type=jnp.float32
    )
    mixture = jnp.sum(mixture * head_mask.astype(jnp.float32)[:, None, :], axis=3)
    return mixture.astype(jnp.bfloat16)


def shards(
    patches,
    level_embed,
    embed_weight,
    block_ids,
    latent_queries,
    cross_gain,
    cross_query,
    cross_kv,
    cross_out,
    region_ids,
    swin_gain,
    swin_qkv,
    swin_out,
    mlp_gain,
    mlp_up,
    mlp_down,
):
    band_count, row_count, col_count, feature_count = patches.shape[1:]
    model_width = embed_weight.shape[1]
    head_dim = model_width // HEADS
    inv_root = 1.0 / math.sqrt(head_dim)
    latent_count = latent_queries.shape[0]
    feature_head = jnp.arange(model_width, dtype=jnp.int32) // head_dim
    head_mask = (feature_head[None, :] == jnp.arange(HEADS, dtype=jnp.int32)[:, None]).astype(
        jnp.bfloat16
    )
    embedded = jnp.dot(
        patches.reshape(-1, feature_count), embed_weight, preferred_element_type=jnp.float32
    )
    embedded = (
        embedded.reshape(band_count, row_count, col_count, model_width) + level_embed[0]
    ).astype(jnp.bfloat16)
    slot_lists = block_ids.reshape(band_count, -1)
    block_index = jnp.arange(row_count, dtype=jnp.int32)
    selector = (slot_lists[:, :, None] == block_index).astype(jnp.bfloat16)
    picked = jnp.einsum(
        "msb,mbwd->mswd", selector, embedded, preferred_element_type=jnp.float32
    ).astype(jnp.bfloat16)
    received, received_ids = (
        lax.all_to_all(picked, "lvl", split_axis=0, concat_axis=0, tiled=True),
        lax.all_to_all(
            slot_lists.astype(jnp.bfloat16), "lvl", split_axis=0, concat_axis=0, tiled=True
        ),
    )
    matches = (received_ids.astype(jnp.int32)[:, :, None] == block_index).astype(jnp.bfloat16)
    tokens = jnp.einsum(
        "lsb,lswd->lbwd", matches, received, preferred_element_type=jnp.float32
    ).astype(jnp.bfloat16)
    presence = jnp.sum(matches.astype(jnp.float32), axis=1)
    level_count = tokens.shape[0]
    cell_count = row_count * col_count
    keys_in = layer_norm(tokens.astype(jnp.float32), cross_gain).astype(jnp.bfloat16)
    level_pairs = jnp.dot(
        keys_in.reshape(-1, model_width), cross_kv, preferred_element_type=jnp.float32
    ).astype(jnp.bfloat16)
    level_keys = level_pairs[:, :model_width]
    level_values = level_pairs[:, model_width:].reshape(level_count, cell_count, model_width)
    cross_queries = (
        jnp.dot(latent_queries, cross_query, preferred_element_type=jnp.float32) * inv_root
    )
    cross_queries = cross_queries.astype(jnp.bfloat16)
    masked_queries = (cross_queries[:, None, :] * head_mask[None]).reshape(-1, model_width)
    scores = jnp.einsum("xd,nd->xn", masked_queries, level_keys, preferred_element_type=jnp.float32)
    scores = scores.reshape(latent_count, HEADS, level_count, cell_count)
    cell_presence = jnp.repeat(presence, col_count, axis=1)
    exponent = jnp.exp(scores) * cell_presence[None, None]
    weights = (exponent / jnp.sum(exponent, axis=2, keepdims=True)).astype(jnp.bfloat16)
    spread_weights = jnp.einsum(
        "qhlp,hd->qlpd", weights, head_mask, preferred_element_type=jnp.float32
    )
    mixture = jnp.sum(spread_weights * level_values.astype(jnp.float32)[None], axis=1)
    mixture = mixture.astype(jnp.bfloat16).reshape(-1, model_width)
    latent_start = jnp.dot(mixture, cross_out, preferred_element_type=jnp.float32).reshape(
        latent_count, row_count, col_count, model_width
    )
    latent_start = latent_queries.astype(jnp.float32)[:, None, None, :] + latent_start
    normed = layer_norm(latent_start, swin_gain).astype(jnp.bfloat16)
    flat_normed = normed.reshape(-1, model_width)
    queries = (
        jnp.dot(flat_normed, swin_qkv[:, :model_width], preferred_element_type=jnp.float32)
        * inv_root
    )
    queries = queries.astype(jnp.bfloat16).reshape(latent_count, row_count, col_count, model_width)
    labels_own = region_ids.astype(jnp.bfloat16)[None]
    row_block = lax.axis_index("lvl") * lax.axis_size("lat") + lax.axis_index("lat")
    parity = row_block % 2
    col_margin = WIN_LAT // 2
    level_pad = WIN_LV // 2
    pair_rows = 2 * row_count
    ext_cols = col_count + 2 * col_margin

    def join_pair(own_part, other_part):
        leading = jnp.concatenate([own_part, other_part], axis=1)
        trailing_first = jnp.concatenate([other_part, own_part], axis=1)
        return jnp.where(parity == 0, leading, trailing_first)

    other_normed, other_labels = from_partner((normed, labels_own), ("lvl", "lat"), 0)
    widened = join_pair(normed, other_normed)
    labels = join_pair(labels_own, other_labels)
    widened, labels = (
        with_halo(widened, (("lon", 2),), col_margin),
        with_halo(labels, (("lon", 2),), col_margin),
    )
    key_value = jnp.dot(
        widened.reshape(-1, model_width),
        swin_qkv[:, model_width:],
        preferred_element_type=jnp.float32,
    ).astype(jnp.bfloat16)
    key_value = key_value.reshape(latent_count, pair_rows, ext_cols, 2 * model_width)
    level_span = latent_count + 2 * level_pad
    key_value = jnp.pad(key_value, ((level_pad, level_pad), (0, 0), (0, 0), (0, 0)))
    window_keys = key_value[:, :, :, :model_width]
    window_values = key_value[:, :, :, model_width:]
    queries = jnp.pad(queries, ((level_pad, level_pad), (0, 0), (col_margin, col_margin), (0, 0)))
    total_cols = lax.axis_size("lon") * col_count
    global_cols = (
        lax.axis_index("lon") * col_count - col_margin + jnp.arange(ext_cols, dtype=jnp.int32)
    )
    col_usable = (global_cols >= 0) & (global_cols < total_cols)
    level_slot = jnp.arange(level_span, dtype=jnp.int32)
    level_usable = (level_slot >= level_pad) & (level_slot < latent_count + level_pad)
    usable = (
        level_usable[:, None, None]
        & col_usable[None, None, :]
        & jnp.ones((1, pair_rows, 1), jnp.bool_)
    )
    key_spans = (WIN_LV, pair_rows, WIN_LAT)
    query_spans = (WIN_LV, row_count, WIN_LAT)
    own_start = parity * row_count
    key_labels = labels[0]
    query_labels = lax.dynamic_slice_in_dim(key_labels, own_start, row_count, 0)
    query_windows = label_windows(query_labels, (row_count, WIN_LAT))
    key_windows = label_windows(key_labels, (pair_rows, WIN_LAT))
    same_label = query_windows[:, :, :, None] == key_windows[:, :, None, :]
    level_pos = jnp.arange(WIN_LV, dtype=jnp.int32)[:, None, None]
    row_pos = jnp.arange(row_count, dtype=jnp.int32)[None, :, None]
    col_pos = jnp.arange(WIN_LAT, dtype=jnp.int32)[None, None, :]
    target = ((level_pos * pair_rows + row_pos + own_start) * WIN_LAT + col_pos).reshape(-1)
    self_pair = (
        target[:, None] == jnp.arange(WIN_LV * pair_rows * WIN_LAT, dtype=jnp.int32)[None, :]
    )
    key_usable = to_windows(usable, key_spans)
    allowed = key_usable[:, :, :, None, :] & same_label[None] | self_pair
    attended_windows = window_attend(
        to_windows(queries, query_spans),
        to_windows(window_keys, key_spans),
        to_windows(window_values, key_spans),
        allowed,
        head_mask,
    )
    attended_windows = from_windows(
        attended_windows, (level_span, row_count, ext_cols), query_spans
    )
    attended_windows = attended_windows[
        level_pad : level_pad + latent_count, :, col_margin : col_margin + col_count
    ]
    attended = jnp.dot(
        attended_windows.reshape(-1, model_width), swin_out, preferred_element_type=jnp.float32
    )
    attended = latent_start + attended.reshape(latent_count, row_count, col_count, model_width)
    mlp_in = layer_norm(attended, mlp_gain).astype(jnp.bfloat16).reshape(-1, model_width)
    hidden = jnp.dot(mlp_in, mlp_up, preferred_element_type=jnp.float32)
    activated = jax.nn.gelu(hidden, approximate=False).astype(jnp.bfloat16)
    lowered = jnp.dot(activated, mlp_down, preferred_element_type=jnp.float32)
    return attended + lowered.reshape(latent_count, row_count, col_count, model_width)


def solution(mesh):
    return jax.shard_map(
        shards,
        mesh=mesh,
        in_specs=(
            P("lvl", None, "lat", "lon", None),
            P("lvl", None),
            P(),
            P("lvl", None, "lat", "lon", None),
            P(),
            P(),
            P(),
            P(),
            P(),
            P(("lvl", "lat"), "lon"),
            P(),
            P(),
            P(),
            P(),
            P(),
            P(),
        ),
        out_specs=P(None, ("lvl", "lat"), "lon", None),
        check_vma=False,
    )
```

profile of v0, /device:TPU:0, one launch (start us, length us, event | category | flops | bytes accessed | tf_op | source)
XLA Modules:
  0.0 129.3 jit_solution(12698198971269133129)
XLA Ops:
  1.4 4.2 %all-to-all-start = ((bf16[2,1,3]{2,1,0:T(2,128)(2,1)}), bf16[2,1,3]{2,1,0:T(2,128)(2,1)S(1)}, u32[]{:S(2)}, u32[]{:S(2)}) async-start(bf16[2,1,3]{2,1,0:T(2,128)(2,1)} %convert_bitcast_fusion.1), calls=%async_computation | async-start | bytes 2048 | tf_op jit(solution)/shard_map/all_to_all | solution.py:135
  6.3 2.0 %collective-permute-start = (bf16[1,6,12]{2,1,0:T(8,128)(2,1)S(1)}, bf16[1,6,12]{2,1,0:T(8,128)(2,1)S(1)}, u32[]{:S(2)}, u32[]{:S(2)}) collective-permute-start(bf16[1,6,12]{2,1,0:T(8,128)(2,1)S(1)} %convert_bitcast_fusion), channel_id=1, source_target_pairs={{0,4},{4,0},{8,12},{12,8},{16,20},{20,16},{24,28},{28,24},{1,5},{5... | collective-permute-start | bytes 440 | tf_op jit(solution)/shard_map/ppermute | solution.py:20
  14.1 3.3 %all-to-all-start.1 = ((bf16[2,3,12,512]{3,1,2,0:T(4,128)(2,1)}), bf16[2,3,12,512]{3,1,2,0:T(4,128)(2,1)S(1)}, u32[]{:S(2)}, u32[]{:S(2)}) async-start(bf16[2,3,12,512]{3,1,2,0:T(4,128)(2,1)} %convolution_convert_fusion.3), calls=%async_computation.1 | async-start | bytes 196608 | tf_op jit(solution)/shard_map/all_to_all | solution.py:134
  20.6 3.3 %collective-permute-done.2 = bf16[1,12,3]{2,1,0:T(8,128)(2,1)S(1)} collective-permute-done((bf16[1,12,3]{2,1,0:T(8,128)(2,1)S(1)}, bf16[1,12,3]{2,1,0:T(8,128)(2,1)S(1)}, u32[]{:S(2)}, u32[]{:S(2)}) %collective-permute-start.2) | collective-permute-done | bytes 104 | tf_op jit(solution)/shard_map/ppermute | solution.py:31
  30.5 8.6 %collective-permute-done.3 = bf16[4,6,12,512]{3,2,1,0:T(8,128)(2,1)} collective-permute-done((bf16[4,6,12,512]{3,2,1,0:T(8,128)(2,1)S(1)}, bf16[4,6,12,512]{3,2,1,0:T(8,128)(2,1)}, u32[]{:S(2)}, u32[]{:S(2)}) %collective-permute-start.3) | collective-permute-done | bytes 294944 | tf_op jit(solution)/shard_map/ppermute | solution.py:20
  42.2 3.8 %collective-permute-start.4 = (bf16[4,12,3,512]{3,2,1,0:T(4,128)(2,1)}, bf16[4,12,3,512]{3,2,1,0:T(4,128)(2,1)}, u32[]{:S(2)}, u32[]{:S(2)}) collective-permute-start(bf16[4,12,3,512]{3,2,1,0:T(4,128)(2,1)} %get-tuple-element.7), channel_id=1, source_target_pairs={{0,1},{1,2},{2,3},{4,5},{5,6},{6,7},{8,9},{9,10},{10,11},{12,13},{... | collective-permute-start | bytes 442376 | tf_op jit(solution)/shard_map/ppermute | solution.py:28
  47.4 2.1 %fusion.21 = bf16[288,512]{1,0:T(8,128)(2,1)} fusion(bf16[288,512]{1,0:T(8,128)(2,1)S(1)} %copy-done.8, bf16[512,1536]{1,0:T(8,128)(2,1)} %param.27), kind=kOutput, calls=%fused_computation.42 | convolution fusion | flops 151289856 | bytes 1114112 | tf_op jit(solution)/shard_map/dot_general | solution.py:174
  51.6 2.2 %reshape.486 = bf16[3,2,1,6,3,6,512]{6,5,4,3,1,0,2:T(8,128)(2,1)} reshape(bf16[6,6,18,512]{3,2,1,0:T(8,128)(2,1)} %pad.8) | data formatting | bytes 1327104 | tf_op jit(solution)/shard_map/reshape | solution.py:47
  58.1 3.0 %pad_maximum_fusion = bf16[4,12,18,512]{3,2,1,0:T(8,128)(2,1)} fusion(bf16[4,12,3,512]{3,2,1,0:T(4,128)(2,1)} %collective-permute-done.5, bf16[4,12,12,512]{3,2,1,0:T(8,128)(2,1)} %copy-done.3, bf16[4,12,3,512]{3,2,1,0:T(4,128)(2,1)} %collective-permute-done.4), kind=kLoop, calls=%fused_computation.45 | loop fusion | flops 2654208 | bytes 1769472 | tf_op jit(solution)/shard_map/concatenate | solution.py:32
  61.1 2.2 %reshape.465 = bf16[864,512]{1,0:T(8,128)(2,1)} reshape(bf16[4,12,18,512]{3,2,1,0:T(8,128)(2,1)} %pad_maximum_fusion) | data formatting | bytes 1769472 | tf_op jit(solution)/shard_map/reshape | solution.py:199
  63.3 3.8 %convolution_convert_fusion = bf16[864,1024]{1,0:T(8,128)(2,1)} fusion(bf16[864,512]{1,0:T(8,128)(2,1)} %reshape.465, bf16[512,1536]{1,0:T(8,128)(2,1)} %param.27), kind=kOutput, calls=%fused_computation.32 | convolution fusion | flops 906854400 | bytes 3702784 | tf_op jit(solution)/shard_map/dot_general | solution.py:198
  67.1 3.8 %reshape.466 = bf16[4,12,18,1024]{3,2,1,0:T(8,128)(2,1)} reshape(bf16[864,1024]{1,0:T(8,128)(2,1)} %convolution_convert_fusion) | data formatting | bytes 3538944 | tf_op jit(solution)/shard_map/reshape | solution.py:203
  70.9 3.8 %pad_slice_fusion = (bf16[6,12,18,512]{3,2,1,0:T(8,128)(2,1)}, bf16[6,12,18,512]{3,2,1,0:T(8,128)(2,1)}) fusion(bf16[4,12,18,1024]{3,2,1,0:T(8,128)(2,1)} %reshape.466), kind=kLoop, calls=%fused_computation.11 | loop fusion | bytes 4423680 | tf_op jit(solution)/shard_map/slice | solution.py:207
  74.7 3.7 %reshape.489 = bf16[3,2,1,12,3,6,512]{6,5,4,3,1,0,2:T(8,128)(2,1)} reshape(bf16[6,12,18,512]{3,2,1,0:T(8,128)(2,1)} %get-tuple-element.5) | data formatting | bytes 2654208 | tf_op jit(solution)/shard_map/reshape | solution.py:47
  78.4 2.8 %copy.79 = bf16[3,2,1,12,3,6,512]{6,1,0,5,4,3,2:T(2,128)(2,1)S(1)} copy(bf16[3,2,1,12,3,6,512]{6,5,4,3,1,0,2:T(8,128)(2,1)} %reshape.489) | data formatting | bytes 2654208 | tf_op jit(solution)/shard_map/reshape | solution.py:47
  82.8 3.5 %reshape.484 = bf16[3,3,144,512,1]{3,2,1,0,4:T(8,128)(2,1)} reshape(bf16[3,1,3,2,12,6,512]{6,5,4,3,2,0,1:T(8,128)(2,1)} %copy.50) | data formatting | bytes 2654208 | tf_op jit(solution)/shard_map/reshape.19
  86.4 3.7 %reshape.487 = bf16[3,2,1,12,3,6,512]{6,5,4,3,1,0,2:T(8,128)(2,1)} reshape(bf16[6,12,18,512]{3,2,1,0:T(8,128)(2,1)} %get-tuple-element.6) | data formatting | bytes 2654208 | tf_op jit(solution)/shard_map/reshape | solution.py:47
  90.1 2.8 %copy.80 = bf16[3,2,1,12,3,6,512]{6,1,0,5,4,3,2:T(2,128)(2,1)S(1)} copy(bf16[3,2,1,12,3,6,512]{6,5,4,3,1,0,2:T(8,128)(2,1)} %reshape.487) | data formatting | bytes 2654208 | tf_op jit(solution)/shard_map/reshape | solution.py:47
  94.5 3.5 %reshape.483 = bf16[3,3,144,512,1]{3,2,1,0,4:T(8,128)(2,1)} reshape(bf16[3,1,3,2,12,6,512]{6,5,4,3,2,0,1:T(8,128)(2,1)} %copy.48) | data formatting | bytes 2654208 | tf_op jit(solution)/shard_map/reshape.15
  98.1 5.8 %fusion.2 = (f32[3,3,16,72]{3,2,1,0:T(8,128)S(1)}, f32[3,3,16,72,144]{4,3,2,1,0:T(8,128)S(1)}) fusion(pred[3,3,72,144]{3,2,1,0:T(8,128)(4,1)} %and_or_fusion, bf16[3,3,144,512,1]{3,2,1,0,4:T(8,128)(2,1)} %reshape.483, bf16[16,512]{1,0:T(8,128)(2,1)} %copy-done.10, bf16[3,3,72,512]{3,2,1,0:T(8,128)(2,1)S(1)} %mul.196), kind=kOutput, calls=%fused_computation.5 | convolution fusion | flops 1537107840 | bytes 8113792 | tf_op jit(solution)/shard_map/abchqd,abckd->abchqk/dot_general | solution.py:82
  103.9 5.1 %multiply_reduce_fusion = bf16[3,3,72,512]{3,2,1,0:T(8,128)(2,1)S(1)} fusion(f32[16,512]{1,0:T(8,128)S(1)} %copy-done.11, f32[3,3,16,72,144]{4,3,2,1,0:T(8,128)S(1)} %get-tuple-element.22, f32[3,3,16,72]{3,2,1,0:T(8,128)S(1)} %get-tuple-element.21, pred[3,3,72,144]{3,2,1,0:T(8,128)(4,1)S(1)} %copy-done.9, bf16[3,3,144,512,1]{3,2,1,0,4:T(8,128)(2,1)S(1)} %copy-done.4), kind=kOutput, calls=%fused_computation | convolution fusion | flops 1543587840 | bytes 8130176 | tf_op jit(solution)/shard_map/abchqk,abckd->abchqd/dot_general | solution.py:87
  110.2 2.2 %copy.66 = bf16[3,2,1,6,3,6,512]{6,5,4,3,1,0,2:T(8,128)(2,1)} copy(bf16[3,2,1,6,3,6,512]{6,5,3,1,4,0,2:T(8,128)(2,1)} %bitcast.110) | data formatting | bytes 1327104 | tf_op jit(solution)/shard_map/reshape | solution.py:67
  112.4 2.2 %reshape.491 = bf16[6,6,18,512]{3,2,1,0:T(8,128)(2,1)} reshape(bf16[3,2,1,6,3,6,512]{6,5,4,3,1,0,2:T(8,128)(2,1)} %copy.66) | data formatting | bytes 1327104 | tf_op jit(solution)/shard_map/reshape | solution.py:67
  118.0 7.9 %fusion.22 = f32[288,512]{1,0:T(8,128)S(1)} fusion(bf16[2048,512]{1,0:T(8,128)(2,1)S(1)} %copy-done, bf16[288,512]{1,0:T(8,128)(2,1)} %reshape.472, bf16[512,2048]{1,0:T(8,128)(2,1)} %param.30), kind=kOutput, calls=%fused_computation.46 | convolution fusion | flops 1246298112 | bytes 5079040 | tf_op jit(solution)/shard_map/dot_general | solution.py:258
  (119 shorter events, 39.3 us)
Async XLA Ops:
  0.0 118.0 %copy-start = (bf16[2048,512]{1,0:T(8,128)(2,1)S(1)}, bf16[2048,512]{1,0:T(8,128)(2,1)}, u32[]{:S(2)}) copy-start(bf16[2048,512]{1,0:T(8,128)(2,1)} %param.31) | copy-start | bytes 6291460
  0.0 13.2 %copy-start.12 = (s32[1,2,1,1,3]{4,3,2,1,0:T(1,128)S(1)}, s32[1,2,1,1,3]{4,3,2,1,0:T(1,128)}, u32[]{:S(2)}) copy-start(s32[1,2,1,1,3]{4,3,2,1,0:T(1,128)} %param.19) | copy-start | bytes 76
  0.0 25.9 %copy-start.14 = (f32[512]{0:T(512)S(1)}, f32[512]{0:T(512)}, u32[]{:S(2)}) copy-start(f32[512]{0:T(512)} %param.21) | copy-start | bytes 6148
  1.4 12.8 %all-to-all-start = ((bf16[2,1,3]{2,1,0:T(2,128)(2,1)}), bf16[2,1,3]{2,1,0:T(2,128)(2,1)S(1)}, u32[]{:S(2)}, u32[]{:S(2)}) async-start(bf16[2,1,3]{2,1,0:T(2,128)(2,1)} %convert_bitcast_fusion.1), calls=%async_computation | async-start | bytes 2048 | tf_op jit(solution)/shard_map/all_to_all | solution.py:135
  6.3 11.4 %collective-permute-start = (bf16[1,6,12]{2,1,0:T(8,128)(2,1)S(1)}, bf16[1,6,12]{2,1,0:T(8,128)(2,1)S(1)}, u32[]{:S(2)}, u32[]{:S(2)}) collective-permute-start(bf16[1,6,12]{2,1,0:T(8,128)(2,1)S(1)} %convert_bitcast_fusion), channel_id=1, source_target_pairs={{0,4},{4,0},{8,12},{12,8},{16,20},{20,16},{24,28},{28,24},{1,5},{5... | collective-permute-start | bytes 440 | tf_op jit(solution)/shard_map/ppermute | solution.py:20
  11.4 15.2 %copy-start.10 = (bf16[16,512]{1,0:T(8,128)(2,1)}, bf16[16,512]{1,0:T(8,128)(2,1)S(1)}, u32[]{:S(2)}) copy-start(bf16[16,512]{1,0:T(8,128)(2,1)S(1)} %get-tuple-element.14) | copy-start | bytes 49156
  11.4 14.7 %copy-start.5 = (bf16[512,1024]{1,0:T(8,128)(2,1)S(1)}, bf16[512,1024]{1,0:T(8,128)(2,1)}, u32[]{:S(2)}) copy-start(bf16[512,1024]{1,0:T(8,128)(2,1)} %param.23) | copy-start | bytes 3145732
  14.1 11.2 %all-to-all-start.1 = ((bf16[2,3,12,512]{3,1,2,0:T(4,128)(2,1)}), bf16[2,3,12,512]{3,1,2,0:T(4,128)(2,1)S(1)}, u32[]{:S(2)}, u32[]{:S(2)}) async-start(bf16[2,3,12,512]{3,1,2,0:T(4,128)(2,1)} %convolution_convert_fusion.3), calls=%async_computation.1 | async-start | bytes 196608 | tf_op jit(solution)/shard_map/all_to_all | solution.py:134
  17.8 2.8 %collective-permute-start.1 = (bf16[1,12,3]{2,1,0:T(8,128)(2,1)S(1)}, bf16[1,12,3]{2,1,0:T(8,128)(2,1)S(1)}, u32[]{:S(2)}, u32[]{:S(2)}) collective-permute-start(bf16[1,12,3]{2,1,0:T(8,128)(2,1)S(1)} %get-tuple-element.11), channel_id=1, source_target_pairs={{0,1},{1,2},{2,3},{4,5},{5,6},{6,7},{8,9},{9,10},{10,11},{12,13},{... | collective-permute-start | bytes 224 | tf_op jit(solution)/shard_map/ppermute | solution.py:28
  19.3 4.6 %collective-permute-start.2 = (bf16[1,12,3]{2,1,0:T(8,128)(2,1)S(1)}, bf16[1,12,3]{2,1,0:T(8,128)(2,1)S(1)}, u32[]{:S(2)}, u32[]{:S(2)}) collective-permute-start(bf16[1,12,3]{2,1,0:T(8,128)(2,1)S(1)} %get-tuple-element.12), channel_id=1, source_target_pairs={{1,0},{2,1},{3,2},{5,4},{6,5},{7,6},{9,8},{10,9},{11,10},{13,12},{... | collective-permute-start | bytes 224 | tf_op jit(solution)/shard_map/ppermute | solution.py:31
  26.2 1.2 copy-start.7
  26.6 1.5 %copy-start.15 = (f32[512]{0:T(512)S(1)}, f32[512]{0:T(512)}, u32[]{:S(2)}) copy-start(f32[512]{0:T(512)} %param.26) | copy-start | bytes 6148
  27.2 1.6 %copy-start.13 = (bf16[3,72]{1,0:T(4,128)(2,1)S(1)}, bf16[3,72]{1,0:T(4,128)(2,1)}, u32[]{:S(2)}) copy-start(bf16[3,72]{1,0:T(4,128)(2,1)} %maximum_bitcast_fusion.1) | copy-start | bytes 1300
  28.3 10.8 %collective-permute-start.3 = (bf16[4,6,12,512]{3,2,1,0:T(8,128)(2,1)S(1)}, bf16[4,6,12,512]{3,2,1,0:T(8,128)(2,1)}, u32[]{:S(2)}, u32[]{:S(2)}) collective-permute-start(bf16[4,6,12,512]{3,2,1,0:T(8,128)(2,1)S(1)} %multiply_convert_fusion.1), channel_id=1, source_target_pairs={{0,4},{4,0},{8,12},{12,8},{16,20},{20,16},{24,28},{28,24},{1,5},{5... | collective-permute-start | bytes 884744 | tf_op jit(solution)/shard_map/ppermute | solution.py:20
  30.5 17.0 %copy-start.8 = (bf16[288,512]{1,0:T(8,128)(2,1)S(1)}, bf16[288,512]{1,0:T(8,128)(2,1)}, u32[]{:S(2)}) copy-start(bf16[288,512]{1,0:T(8,128)(2,1)} %reshape.462) | copy-start | bytes 884740
  40.3 0.9 copy-start.3
  42.2 15.9 %collective-permute-start.4 = (bf16[4,12,3,512]{3,2,1,0:T(4,128)(2,1)}, bf16[4,12,3,512]{3,2,1,0:T(4,128)(2,1)}, u32[]{:S(2)}, u32[]{:S(2)}) collective-permute-start(bf16[4,12,3,512]{3,2,1,0:T(4,128)(2,1)} %get-tuple-element.7), channel_id=1, source_target_pairs={{0,1},{1,2},{2,3},{4,5},{5,6},{6,7},{8,9},{9,10},{10,11},{12,13},{... | collective-permute-start | bytes 442376 | tf_op jit(solution)/shard_map/ppermute | solution.py:28
  46.0 12.1 %collective-permute-start.5 = (bf16[4,12,3,512]{3,2,1,0:T(4,128)(2,1)}, bf16[4,12,3,512]{3,2,1,0:T(4,128)(2,1)}, u32[]{:S(2)}, u32[]{:S(2)}) collective-permute-start(bf16[4,12,3,512]{3,2,1,0:T(4,128)(2,1)} %get-tuple-element.8), channel_id=1, source_target_pairs={{1,0},{2,1},{3,2},{5,4},{6,5},{7,6},{9,8},{10,9},{11,10},{13,12},{... | collective-permute-start | bytes 442376 | tf_op jit(solution)/shard_map/ppermute | solution.py:31
  98.1 5.8 %copy-start.4 = (bf16[3,3,144,512,1]{3,2,1,0,4:T(8,128)(2,1)S(1)}, bf16[3,3,144,512,1]{3,2,1,0,4:T(8,128)(2,1)}, u32[]{:S(2)}) copy-start(bf16[3,3,144,512,1]{3,2,1,0,4:T(8,128)(2,1)} %reshape.484) | copy-start | bytes 3981316
  98.1 5.8 %copy-start.9 = (pred[3,3,72,144]{3,2,1,0:T(8,128)(4,1)S(1)}, pred[3,3,72,144]{3,2,1,0:T(8,128)(4,1)}, u32[]{:S(2)}) copy-start(pred[3,3,72,144]{3,2,1,0:T(8,128)(4,1)} %and_or_fusion) | copy-start | bytes 279940
  98.1 5.9 %copy-start.11 = (f32[16,512]{1,0:T(8,128)S(1)}, f32[16,512]{1,0:T(8,128)}, u32[]{:S(2)}) copy-start(f32[16,512]{1,0:T(8,128)} %get-tuple-element.13) | copy-start | bytes 98308
  110.2 4.4 %copy-start.6 = (bf16[512,512]{1,0:T(8,128)(2,1)S(1)}, bf16[512,512]{1,0:T(8,128)(2,1)}, u32[]{:S(2)}) copy-start(bf16[512,512]{1,0:T(8,128)(2,1)} %param.28) | copy-start | bytes 1572868
  112.4 4.6 %copy-start.16 = (f32[512]{0:T(512)S(1)}, f32[512]{0:T(512)}, u32[]{:S(2)}) copy-start(f32[512]{0:T(512)} %param.29) | copy-start | bytes 6148
  118.0 8.8 %copy-start.2 = (f32[4,6,12,512]{3,2,1,0:T(8,128)S(1)}, f32[4,6,12,512]{3,2,1,0:T(8,128)}, u32[]{:S(2)}) copy-start(f32[4,6,12,512]{3,2,1,0:T(8,128)} %copy-done.1) | copy-start | bytes 1769476
  (1 other events, 0.9 us)
where the time goes:
time: 131 us; the launch traced here: 129 us
  local copies, waits for them, and re-layouts  54.7 us (42%)
  matrix products  31.8 us (24%)
  starting transfers between devices  18.1 us (14%)
  other arithmetic  12.3 us (9%)
  waiting for transfers between devices  11.9 us (9%)
    reshape x6, local copies, waits for them, and re-layouts, to_windows(): tensor.reshape((level_span // first, first, row_span // second, second, c...  17.1 us
    ppermute x2, waiting for transfers between devices, from_partner(): return lax.ppermute(block, axis, route)  8.59 us
    dot_general x1, matrix products, shards(): lowered = jnp.dot(activated, mlp_down, preferred_element_type=jnp.float32)  7.86 us
    another operation x2, local copies, waits for them, and re-layouts  7.06 us
    dot_general x1, matrix products, window_attend(): jnp.einsum('abchqd,abckd->abchqk', masked, key_rows, preferred_element_ty...  5.83 us
    ppermute x2, starting transfers between devices, with_halo(): lax.ppermute(lax.slice_in_dim(block, block.shape[dim] - width, None, axis...  5.25 us
    dot_general x1, matrix products, window_attend(): jnp.einsum('abchqk,abckd->abchqd', weights, value_rows, preferred_element...  5.09 us
    reshape x2, local copies, waits for them, and re-layouts, from_windows(): shaped.transpose(axes_order)  4.38 us
  transfers between devices with their start and end apart: 8, of which 2 were waited for; matrix products, arithmetic and copies ran while one was open for 16% of the time, Pallas kernels for 0%

commit v1 on v0

v1 whole, which is shorter than its diff:
```python
import functools
import math

import jax
import jax.numpy as jnp
import numpy as np
from jax import lax
from jax.experimental import pallas as pl
from jax.experimental.pallas import tpu as pltpu
from jax.sharding import PartitionSpec as P

HEADS = 16
WIN_LAT = 6
BLOCK = 16
CODE = 64
MESH = pl.DeviceIdType.MESH
F32 = jnp.float32
BF16 = jnp.bfloat16


def layer_norm(tensor, gain_vec):
    average = jnp.mean(tensor, axis=-1, keepdims=True)
    centred = tensor - average
    spread = jnp.mean(centred * centred, axis=-1, keepdims=True)
    return centred * lax.rsqrt(spread + 1e-05) * gain_vec


def mm(a, b):
    return jnp.dot(a, b, preferred_element_type=F32)


def mm_nt(a, b):
    return lax.dot_general(a, b, (((1,), (1,)), ((), ())), preferred_element_type=F32)


class Plan:
    def __init__(self, rows, cols, cap):
        self.rows, self.cols, self.cap = rows, cols, cap
        self.margin = WIN_LAT // 2
        per = (BLOCK - 1) // cap
        assert per >= self.margin and rows < CODE and rows * cols <= 128
        self.blocks = max(2, -(-cols // per))
        spread = [min(per, cols)]
        middle = cols - 2 * per
        assert middle >= 0
        groups = [list(range(per))]
        groups += [list(range(c, min(c + per, cols - per))) for c in range(per, cols - per, per)]
        groups += [list(range(cols - per, cols))]
        self.blocks = len(groups)
        self.tile_rows = self.blocks * BLOCK
        col_of = np.full((self.blocks, BLOCK), -1)
        for b, group in enumerate(groups):
            for k, c in enumerate(group):
                col_of[b, k * cap : (k + 1) * cap] = c
        self.col_of = col_of.reshape(-1)
        self.tiles = [(0, self.tile_rows), (self.tile_rows, self.tile_rows)]
        self.tiles += [(2 * self.tile_rows + k * BLOCK, BLOCK) for k in range(4)]
        self.wide_rows = 2 * self.tile_rows + 4 * BLOCK
        first, last = self.col_of[:BLOCK], self.col_of[-BLOCK:]
        parts = [self.col_of, self.col_of, last, last, first, first]
        row_code = np.concatenate(
            [np.where(p >= 0, (t * cols + p) * CODE, -100000) for t, p in enumerate(parts)]
        )
        lanes = -(-self.wide_rows // 128) * 128
        self.lanes = lanes
        self.row_code = np.full((8, lanes), -100000, np.int32)
        self.row_code[:, : self.wide_rows] = row_code
        m = self.margin
        spans = [range(cols), range(cols), range(cols - m, cols), range(cols - m, cols), range(m), range(m)]
        offset = [0, 0, -cols, -cols, cols, cols]
        cells = [(t, i, j, (j + offset[t] + m) // WIN_LAT) for t in range(6) for i in range(rows) for j in spans[t]]
        self.cells = np.array(cells)
        self.count = len(cells)
        self.own = rows * cols
        self.info = np.zeros((self.count, 128), np.int32)
        t, i, j, win = self.cells.T
        self.info[:, 0] = (t * cols + j) * CODE + i
        self.info[:, 1] = i * cols + j
        self.info[:, 2] = t
        self.win = (win[: self.own, None] == win[None, :]).astype(np.float32)


def send_kernel(plan, names, sizes, patches, level_embed, weight, ids, labels, out, wbuf, buf, wsem, send, recv, local):
    rows, cols, cap = plan.rows, plan.cols, plan.cap
    levels, lat_count, lon_count = sizes
    width = weight.shape[1]
    load = pltpu.make_async_copy(weight, wbuf, wsem)
    load.start()
    me_l, me_a, me_o = (lax.axis_index(name) for name in names)
    low_bit = lax.rem(me_a, 2)
    partner = me_a + 1 - 2 * low_bit
    lats = (me_a, partner)
    lons = {
        0: me_o,
        1: lax.rem(me_o + 1, lon_count),
        -1: lax.rem(me_o + lon_count - 1, lon_count),
    }
    moves = [
        (dm, da, do)
        for dm in range(levels)
        for da in (0, 1)
        for do in (0, -1, 1)
        if (dm, da, do) != (0, 0, 0)
    ]
    band_of = [lax.rem(me_l + dm, levels) for dm in range(levels)]
    barrier = pltpu.get_barrier_semaphore()
    for dm, da, do in moves:
        pl.semaphore_signal(
            barrier, inc=1, device_id=(band_of[dm], lats[da], lons[do]), device_id_type=MESH
        )

    tile_rows = plan.tile_rows
    row = lax.broadcasted_iota(jnp.int32, (tile_rows, 1), 0)
    col_of = jnp.full((tile_rows, 1), -1, jnp.int32)
    slot_of = jnp.full((tile_rows, 1), -1, jnp.int32)
    for r in range(tile_rows):
        pass
    in_block = jnp.bitwise_and(row, BLOCK - 1)
    base = jnp.zeros((tile_rows, 1), jnp.int32)
    for b in range(plan.blocks):
        start = int(plan.col_of[b * BLOCK])
        base = jnp.where((row >= b * BLOCK) & (row < (b + 1) * BLOCK), start, base)
    col_step = jnp.zeros((tile_rows, 1), jnp.int32)
    for k in range(1, BLOCK // cap + 1):
        col_step = col_step + (in_block >= k * cap).astype(jnp.int32)
    slot_of = in_block - col_step * cap
    col_of = base + col_step
    used = jnp.zeros((tile_rows, 1), jnp.bool_)
    for b in range(plan.blocks):
        n = int((plan.col_of[b * BLOCK : (b + 1) * BLOCK] >= 0).sum())
        used = used | ((row >= b * BLOCK) & (row < b * BLOCK + n))
    cell = lax.broadcasted_iota(jnp.int32, (128, 1), 0)
    cell_i = jnp.zeros((128, 1), jnp.int32)
    for k in range(1, rows):
        cell_i = cell_i + (cell >= k * cols).astype(jnp.int32)
    cell_j = cell - cell_i * cols
    lab = labels[...].astype(F32)
    col_lab = jnp.zeros((128, cols), F32)
    for k in range(rows):
        col_lab = jnp.where(cell_i == k, lab[k : k + 1, :], col_lab)
    picked_j = lax.broadcasted_iota(jnp.int32, (128, cols), 1) == cell_j
    lab_col = jnp.sum(jnp.where(picked_j, col_lab, 0.0), axis=1, keepdims=True)
    eye = lax.broadcasted_iota(jnp.int32, (128, 128), 0) == lax.broadcasted_iota(jnp.int32, (128, 128), 1)
    lab_row = jnp.sum(jnp.where(eye, lab_col, 0.0), axis=0, keepdims=True)
    lane = lax.broadcasted_iota(jnp.int32, (1, plan.lanes), 1)
    lane_in = jnp.bitwise_and(lane, BLOCK - 1)
    lane_step = jnp.zeros_like(lane)
    for k in range(1, BLOCK // cap + 1):
        lane_step = lane_step + (lane_in >= k * cap).astype(jnp.int32)
    lane_slot = lane_in - lane_step * cap

    picked, metas = [], []
    for band in range(levels):
        id_col = jnp.full((tile_rows, 1), -1, jnp.int32)
        id_row = jnp.full((1, plan.lanes), -1, jnp.int32)
        for s in range(cap):
            number = ids[0, band, 0, 0, s]
            id_col = jnp.where(slot_of == s, number, id_col)
            id_row = jnp.where(lane_slot == s, number, id_row)
        id_col = jnp.where(used, id_col, -1)
        same_col = (lax.broadcasted_iota(jnp.int32, (tile_rows, cols), 1) == col_of) & used
        total = jnp.zeros((tile_rows, patches.shape[-1]), F32)
        for i in range(rows):
            chosen = jnp.where(same_col & (id_col == i), 1.0, 0.0).astype(BF16)
            total = total + mm(chosen, patches[0, band, i])
        picked.append(total)
        pad = jnp.zeros((1, width - plan.lanes - 128), F32)
        metas.append(jnp.concatenate([id_row.astype(F32), lab_row, pad], axis=1))
    stacked = jnp.concatenate(picked, axis=0).astype(BF16)
    load.wait()
    embedded = mm(stacked, wbuf[...]) + level_embed[...]
    for band in range(levels):
        part = embedded[band * tile_rows : (band + 1) * tile_rows]
        buf[band] = jnp.where(in_block == BLOCK - 1, metas[band], part).astype(BF16)
    pl.semaphore_wait(barrier, len(moves))
    copies = []
    for k, (dm, da, do) in enumerate(moves):
        if do == 0:
            source, target, count = 0, plan.tiles[da][0], tile_rows
        elif do == 1:
            source, target, count = tile_rows - BLOCK, plan.tiles[2 + da][0], BLOCK
        else:
            source, target, count = 0, plan.tiles[4 + da][0], BLOCK
        copies.append(
            pltpu.make_async_remote_copy(
                src_ref=buf.at[band_of[dm], pl.ds(source, count)],
                dst_ref=out.at[me_l, pl.ds(target, count)],
                send_sem=send.at[k],
                recv_sem=recv.at[k],
                device_id=(band_of[dm], lats[da], lons[do]),
                device_id_type=MESH,
            )
        )
    for copy in copies[::-1]:
        copy.start()
    own = pltpu.make_async_copy(buf.at[me_l], out.at[me_l, pl.ds(0, tile_rows)], local)
    own.start()
    own.wait()
    for copy in copies:
        copy.wait()


def main_kernel(
    plan, names, sizes, wide, info, row_code, win, hm, lq, cross_gain, swin_gain, mlp_gain,
    cross_kv, cross_query, cross_out, swin_qkv, swin_out, mlp_up, mlp_down,
    out,
    b_kv, b_query, b_out, b_qkv, b_so, b_up, b_down, start, sems,
):
    levels, _, lon_count = sizes
    pairs = [
        (cross_query, b_query), (cross_kv, b_kv), (cross_out, b_out), (swin_qkv, b_qkv),
        (swin_out, b_so), (mlp_up, b_up), (mlp_down, b_down),
    ]
    loads = [pltpu.make_async_copy(a, b, sems.at[k]) for k, (a, b) in enumerate(pairs)]
    for load in loads:
        load.start()
    l_query, l_kv, l_out, l_qkv, l_so, l_up, l_down = loads
    me_l, me_o = lax.axis_index(names[0]), lax.axis_index(names[2])
    width = lq.shape[1]
    head_dim = width // HEADS
    inv_root = 1.0 / math.sqrt(head_dim)
    latents = lq.shape[0]
    own, count = plan.own, plan.count
    lanes = plan.lanes
    code_c = info[:, 0:1]
    pos_c = info[:, 1:2]
    tile_c = info[:, 2:3]
    lane = lax.broadcasted_iota(jnp.int32, (1, lanes), 1)
    meta_rows = [first + BLOCK - 1 for first, _ in plan.tiles]

    lq_f = lq[...].astype(F32)
    l_query.wait()
    cq = (mm(lq[...], b_query[...]) * inv_root).astype(BF16).astype(F32)
    hm_f = hm[...].astype(F32)
    masked = jnp.concatenate([cq[q : q + 1] * hm_f for q in range(latents)], axis=0).astype(BF16)

    l_kv.wait()
    keys, values, presence = [], [], []
    for level in range(levels):
        tokens = wide[level].astype(F32)
        keys_in = layer_norm(tokens, cross_gain[...]).astype(BF16)
        pair = mm(keys_in, b_kv[...]).astype(BF16)
        id_row = tokens[meta_rows[0] : meta_rows[0] + 1, :lanes]
        for t in range(1, 6):
            first, _ = plan.tiles[t]
            id_row = jnp.where(lane >= first, tokens[meta_rows[t] : meta_rows[t] + 1, :lanes], id_row)
        code_r = (row_code[0:1, :] + id_row.astype(jnp.int32))[:, : plan.wide_rows]
        scatter = jnp.where(
            (code_c == code_r) & (id_row.astype(jnp.int32)[:, : plan.wide_rows] >= 0), 1.0, 0.0
        )
        presence.append(jnp.sum(scatter, axis=1, keepdims=True))
        spread = mm(scatter.astype(BF16), pair)
        keys.append(spread[:, :width].astype(BF16))
        values.append(spread[:, width:])
    lab_src = wide[me_l].astype(F32)
    seg = jnp.zeros((count, 128), F32)
    for t in range(6):
        seg = jnp.where(tile_c == t, lab_src[meta_rows[t] : meta_rows[t] + 1, lanes : lanes + 128], seg)
    at_pos = lax.broadcasted_iota(jnp.int32, (count, 128), 1) == pos_c
    lab_col = jnp.sum(jnp.where(at_pos, seg, 0.0), axis=1, keepdims=True)
    eye = lax.broadcasted_iota(jnp.int32, (count, count), 0) == lax.broadcasted_iota(
        jnp.int32, (count, count), 1
    )
    lab_row = jnp.sum(jnp.where(eye, lab_col, 0.0), axis=0, keepdims=True)
    cell_lane = lax.broadcasted_iota(jnp.int32, (1, count), 1)
    halo = (count - 2 * own) // 2
    bad = ((cell_lane >= 2 * own) & (cell_lane < 2 * own + halo) & (me_o == 0)) | (
        (cell_lane >= 2 * own + halo) & (me_o == lon_count - 1)
    )
    lab_row = jnp.where(bad, -1.0, lab_row)
    allowed = jnp.where(lab_col[:own] == lab_row, win[...], 0.0)
    group = 128 // head_dim
    allowed = jnp.concatenate([allowed] * group, axis=0) > 0.5

    exps = [jnp.exp(mm_nt(keys[l], masked)) * presence[l] for l in range(levels)]
    norm = exps[0]
    for e in exps[1:]:
        norm = norm + e
    weights = [(e / norm).astype(BF16) for e in exps]
    hm_all = jnp.concatenate([hm_f] * latents, axis=0)
    hm_row = lax.broadcasted_iota(jnp.int32, hm_all.shape, 0)
    l_out.wait()
    l_qkv.wait()
    queries, wkeys, wvalues = [], [], []
    for q in range(latents):
        expand = jnp.where(
            (hm_row >= q * HEADS) & (hm_row < (q + 1) * HEADS), hm_all, 0.0
        ).astype(BF16)
        mix = mm(weights[0], expand) * values[0]
        for l in range(1, levels):
            mix = mix + mm(weights[l], expand) * values[l]
        latent = mm(mix.astype(BF16), b_out[...]) + lq_f[q : q + 1]
        start[q * own : (q + 1) * own] = latent[:own]
        normed_f = layer_norm(latent, swin_gain[...])
        normed = normed_f.astype(BF16)
        kv = mm(normed, b_qkv[:, width:]).astype(BF16)
        wkeys.append(kv[:, :width])
        wvalues.append(kv[:, width:])
        queries.append(normed_f[:own])
    q_all = mm(jnp.concatenate(queries, axis=0).astype(BF16), b_qkv[:, :width]) * inv_root
    lane_head = [
        (lax.broadcasted_iota(jnp.int32, (1, 128), 1) >= h * head_dim)
        & (lax.broadcasted_iota(jnp.int32, (1, 128), 1) < (h + 1) * head_dim)
        for h in range(group)
    ]
    mixes = []
    for p in range(latents):
        partners = [k for k in range(latents) if (k + 1) // 2 == (p + 1) // 2]
        pieces = []
        for g in range(width // 128):
            cut = slice(g * 128, (g + 1) * 128)
            part = q_all[p * own : (p + 1) * own, cut]
            stack = jnp.concatenate([jnp.where(h, part, 0.0) for h in lane_head], axis=0).astype(BF16)
            raised = [
                jnp.where(allowed, jnp.exp(mm_nt(stack, wkeys[k][:, cut])), 0.0) for k in partners
            ]
            norm = jnp.sum(raised[0], axis=1, keepdims=True)
            for e in raised[1:]:
                norm = norm + jnp.sum(e, axis=1, keepdims=True)
            inverse = 1.0 / norm
            total = mm((raised[0] * inverse).astype(BF16), wvalues[partners[0]][:, cut])
            for e, k in zip(raised[1:], partners[1:]):
                total = total + mm((e * inverse).astype(BF16), wvalues[k][:, cut])
            piece = jnp.zeros((own, 128), F32)
            for h in range(group):
                piece = jnp.where(lane_head[h], total[h * own : (h + 1) * own], piece)
            pieces.append(piece)
        mixes.append(jnp.concatenate(pieces, axis=1))
    l_so.wait()
    attended = start[...] + mm(jnp.concatenate(mixes, axis=0).astype(BF16), b_so[...])
    mlp_in = layer_norm(attended, mlp_gain[...]).astype(BF16)
    l_up.wait()
    l_down.wait()
    hidden = mlp_up.shape[1]
    result = attended
    step = 512
    for c in range(0, hidden, step):
        up = mm(mlp_in, b_up[:, c : c + step])
        act = (up * (1.0 + lax.erf(up * math.sqrt(0.5))) * 0.5).astype(BF16)
        result = result + mm(act, b_down[c : c + step, :])
    rows, cols = plan.rows, plan.cols
    for p in range(latents):
        for i in range(rows):
            first = (p * rows + i) * cols
            out[p, i] = result[first : first + cols]


def shards(
    sizes, names,
    patches, level_embed, embed_weight, block_ids, latent_queries, cross_gain, cross_query, cross_kv,
    cross_out, region_ids, swin_gain, swin_qkv, swin_out, mlp_gain, mlp_up, mlp_down,
):
    levels = sizes[0]
    _, bands, rows, cols, _ = patches.shape
    width = embed_weight.shape[1]
    plan = Plan(rows, cols, block_ids.shape[-1])
    vmem = pl.BlockSpec(memory_space=pltpu.VMEM)
    hbm = pl.BlockSpec(memory_space=pl.ANY)
    moves = 6 * levels - 1
    wide = pl.pallas_call(
        functools.partial(send_kernel, plan, names, sizes),
        out_shape=jax.ShapeDtypeStruct((levels, plan.wide_rows, width), BF16),
        in_specs=[vmem, vmem, hbm, pl.BlockSpec(memory_space=pltpu.SMEM), vmem],
        out_specs=vmem,
        scratch_shapes=[
            pltpu.VMEM(embed_weight.shape, BF16),
            pltpu.VMEM((bands, plan.tile_rows, width), BF16),
            pltpu.SemaphoreType.DMA,
            pltpu.SemaphoreType.DMA((moves,)),
            pltpu.SemaphoreType.DMA((moves,)),
            pltpu.SemaphoreType.DMA,
        ],
        compiler_params=pltpu.CompilerParams(collective_id=0, has_side_effects=True),
        name="send",
    )(patches, level_embed, embed_weight, block_ids, region_ids)
    latents = latent_queries.shape[0]
    head_mask = (np.arange(width)[None, :] // (width // HEADS) == np.arange(HEADS)[:, None])
    weights = (cross_kv, cross_query, cross_out, swin_qkv, swin_out, mlp_up, mlp_down)
    return pl.pallas_call(
        functools.partial(main_kernel, plan, names, sizes),
        out_shape=jax.ShapeDtypeStruct((latents, rows, cols, width), F32),
        in_specs=[vmem] * 9 + [hbm] * 7,
        out_specs=vmem,
        scratch_shapes=[pltpu.VMEM(w.shape, BF16) for w in weights]
        + [pltpu.VMEM((latents * plan.own, width), F32), pltpu.SemaphoreType.DMA((7,))],
        compiler_params=pltpu.CompilerParams(vmem_limit_bytes=56 << 20),
        name="main",
    )(
        wide, jnp.asarray(plan.info), jnp.asarray(plan.row_code), jnp.asarray(plan.win),
        jnp.asarray(head_mask, BF16), latent_queries, cross_gain.reshape(1, -1),
        swin_gain.reshape(1, -1), mlp_gain.reshape(1, -1), *weights,
    )


def solution(mesh):
    names = ("lvl", "lat", "lon")
    sizes = tuple(mesh.shape[name] for name in names)
    tiled = P("lvl", None, "lat", "lon", None)
    return jax.shard_map(
        functools.partial(shards, sizes, names),
        mesh=mesh,
        in_specs=(
            tiled, P("lvl", None), P(), tiled, P(), P(), P(), P(), P(), P(("lvl", "lat"), "lon"),
            P(), P(), P(), P(), P(), P(),
        ),
        out_specs=P(None, ("lvl", "lat"), "lon", None),
        check_vma=False,
    )
```

time: 131 us -> 29.8 us (0.23); the launches traced: 129 us -> 29.5 us
  local copies, waits for them, and re-layouts: 54.7 us -> 4.11 us
  matrix products: 31.8 us -> 0 us
  Pallas kernels: 0 us -> 25.4 us
  starting transfers between devices: 18.1 us -> 0 us
  other arithmetic: 12.3 us -> 0 us
  waiting for transfers between devices: 11.9 us -> 0 us
    dot_general x14 -> x0, matrix products: 31.8 us -> none  [the longest x1 7.86 us: shards(): lowered = jnp.dot(activated, mlp_down, preferred_element_type=jnp.float32)]
    reshape x18 -> x0, local copies, waits for them, and re-layouts: 31.4 us -> none  [the longest x6 17.1 us: to_windows(): tensor.reshape((level_span // first, first, row_span // second, second, c...]
    pallas_call x0 -> x2, Pallas kernels: none -> 25.4 us  [the longest x1 13.4 us: shards(): pl.pallas_call(functools.partial(main_kernel, plan, names, sizes), out_sh...]
    ppermute x6 -> x0, waiting for transfers between devices: 11.9 us -> none  [the longest x2 8.59 us: from_partner(): return lax.ppermute(block, axis, route)]
    ppermute x6 -> x0, starting transfers between devices: 10.5 us -> none  [the longest x2 5.25 us: with_halo(): lax.ppermute(lax.slice_in_dim(block, block.shape[dim] - width, None, axis...]
    all_to_all x2 -> x0, starting transfers between devices: 7.58 us -> none  [the longest x1 4.24 us: shards(): lax.all_to_all(slot_lists.astype(jnp.bfloat16), 'lvl', split_axis=0, conc...]
    another operation x3 -> x0, local copies, waits for them, and re-layouts: 7.08 us -> none
    slice x4 -> x0, local copies, waits for them, and re-layouts: 4.81 us -> none  [the longest x1 3.79 us: shards(): window_values = key_value[:, :, :, model_width:]]
  transfers between devices with their start and end apart: 8 -> 0, of which waited for: 2 -> 0; matrix products, arithmetic and copies ran while one was open for 16% -> 0% of each run, Pallas kernels for 0% -> 0%
where the time goes in v1:
time: 29.8 us; the launch traced here: 29.5 us
  Pallas kernels  25.4 us (85%)
  local copies, waits for them, and re-layouts  4.11 us (14%)
    pallas_call x1, Pallas kernels, shards(): pl.pallas_call(functools.partial(main_kernel, plan, names, sizes), out_sh...  13.4 us
    pallas_call x1, Pallas kernels, shards(): pl.pallas_call(functools.partial(send_kernel, plan, names, sizes), out_sh...  12 us
    pallas_call x1, local copies, waits for them, and re-layouts, shards(): pl.pallas_call(functools.partial(main_kernel, plan, names, sizes), out_sh...  2.33 us
    unnamed x1, local copies, waits for them, and re-layouts  1.78 us

profile of v1, /device:TPU:0, one launch (start us, length us, event | category | flops | bytes accessed | tf_op | source)
XLA Modules:
  0.0 29.5 jit_solution(4603642045420261533)
XLA Ops:
  0.0 1.8 %copy.21.patches = bf16[1,2,6,12,1000]{4,3,2,1,0:T(8,128)(2,1)} copy(bf16[1,2,6,12,1000]{4,1,3,2,0:T(2,128)(2,1)} %param.20) | data formatting | bytes 576000 | tf_op args[0]
  1.8 12.0 %send.1.wide = bf16[2,160,512]{2,1,0:T(8,128)(2,1)} custom-call(bf16[1,2,6,12,1000]{4,3,2,1,0:T(8,128)(2,1)} %copy.21.patches, f32[1,512]{1,0:T(1,128)} %level_embed.1, bf16[1000,512]{1,0:T(8,128)(2,1)} %weight.1, s32[1,2,1,1,3]{4,3,2,1,0:T(1,128)} %ids.1, s32[6,12]{1,0:T(8,128)} %labels.1), custom_call_target="tpu_custom_call" | custom-call | tf_op jit(solution)/shard_map/send/pallas_call | solution.py:360
  13.8 13.4 %main.1 = f32[4,6,12,512]{3,2,1,0:T(8,128)} custom-call(bf16[2,160,512]{2,1,0:T(8,128)(2,1)} %send.1.wide, s32[216,128]{1,0:T(8,128)} %constant.8.clone.info, s32[8,256]{1,0:T(8,128)} %constant.9.clone.row_code, f32[72,216]{1,0:T(8,128)} %constant.10.clone.win, bf16[16,512]{1,0:T(8,128)(2,1)} %constant.11.clone.hm, bf16[4,512]{1,0:T(4,128)(2,1)} %lq.1, ...), custom_call_target="tpu_custom_call" | custom-call | tf_op jit(solution)/shard_map/main/pallas_call | solution.py:379
  27.2 2.3 %copy.22 = f32[4,6,12,512]{3,0,2,1:T(4,128)} copy(f32[4,6,12,512]{3,2,1,0:T(8,128)} %main.1) | data formatting | bytes 1179648 | tf_op jit(solution)/shard_map/main/pallas_call | solution.py:379
